TPU v7x, 32 devices: a whole 2x2x4 slice. The times are simulated.
32 devices in a mesh: groups: 2 (over x), seq: 16 (over z, y, core).
Axes of the slice: x: 2, y: 2, z: 4, core: 2. Of those that a mesh axis runs over, the one named last changes fastest.
Arguments:
- queries: bfloat16 [32, 32, 1024], P('seq', 'groups'), parts along dimension 1, may hold values from -1100 to 1100
- keys: bfloat16 [32, 32, 128], P('seq', 'groups'), parts along dimension 1, may hold values from -4 to 4
- values: bfloat16 [32, 32, 128], P('seq', 'groups'), parts along dimension 1, may hold values from -6 to 6
- cache_keys: bfloat16 [32, 2048, 128], P(('groups', 'seq')), parts along dimension 0, may hold values from -4 to 4
- cache_values: bfloat16 [32, 2048, 128], P(('groups', 'seq')), parts along dimension 0, may hold values from -6 to 6
- cache_len: int32 [32, 16], P(None, 'groups'), parts along dimension 1, may hold values from 1 to 2048, as said below
- out_weight: bfloat16 [2048, 2048], P('seq'), may hold values from -0.5 to 0.5
- norm_gain: bfloat16 [2048], replicated, may hold values from 0.5 to 1.5
- expert_ids: int32 [32, 16, 8], P('seq', 'groups'), parts along dimension 1, may hold values from 0 to 31, all different within a row; in each aligned block of 16 rows (0 to 15, 16 to 31, ..., all dimensions but the last counted through in order) at most 5 rows name the same one
- route_weights: float32 [32, 16, 8], P('seq', 'groups'), parts along dimension 1, may hold values from 0.02 to 1
- w_gate: bfloat16 [32, 2048, 384], P('seq'), may hold values from -0.125 to 0.125
- w_up: bfloat16 [32, 2048, 384], P('seq'), may hold values from -0.125 to 0.125
- w_down: bfloat16 [32, 384, 2048], P('seq'), may hold values from -0.3125 to 0.3125
Outputs:
- projected: bfloat16 [32, 16, 2048], P('seq', 'groups'), parts along dimension 1
- moe_out: bfloat16 [32, 16, 2048], P('seq', 'groups'), parts along dimension 1
There are 2 independent parts, one for each index of `groups`. A program takes and returns all parts, laid end to end along the dimension named above; an argument that names none is the same for every part. Nothing has to cross between parts.
Inputs may be any that keep to these rules, and one draw needn't show every extreme that they name: `cache_len`: every new token sees at least one cached key; some token sees all 2048. `expert_ids`: rows are taken position-major over members; in each aligned block of 16 rows (the rows of one index of seq) no expert is named more than 5 times, a bound that some block reaches.
All inputs are finite; a program needn't handle non-finite values.
Results may differ from a plain program's by a relative error of at most 0.01.
Values may be sent and summed in bfloat16 or wider, within the bound.
No kernel may reach another device: no remote copies, remote signals or barrier semaphores. Data moves between devices by JAX's collectives and lax.ppermute only.
A program may use at most 64 MiB of HBM per device.

v0:
```python
import jax
import jax.numpy as jnp
from jax import lax
from jax.sharding import PartitionSpec as P

D = 2048
HD = 128
TOPK = 8
QH = 16
KVH = 2
CAP = 5


def attend(query_heads, key_rows, value_rows, lengths):
    new_count = query_heads.shape[0]
    cache_count = key_rows.shape[0] - new_count
    scores = jnp.einsum(
        "qhd,kd->hqk", query_heads, key_rows, preferred_element_type=jnp.float32
    ) * HD ** (-0.5)
    cached_ok = jnp.arange(cache_count, dtype=jnp.int32)[None, :] < lengths[:, None]
    causal_ok = (
        jnp.arange(new_count, dtype=jnp.int32)[None, :]
        <= jnp.arange(new_count, dtype=jnp.int32)[:, None]
    )
    visible = jnp.concatenate([cached_ok, causal_ok], axis=1)
    scores = jnp.where(visible[None], scores, -1e30)
    row_max = jnp.max(scores, axis=-1, keepdims=True)
    expo = jnp.exp(scores - row_max)
    row_sum = jnp.sum(expo, axis=-1, keepdims=True)
    weights = (expo / row_sum).astype(jnp.bfloat16)
    result = jnp.einsum("hqk,kd->qhd", weights, value_rows, preferred_element_type=jnp.float32)
    return result.astype(jnp.bfloat16).reshape(new_count, -1)


def body(
    queries,
    keys,
    values,
    cache_keys,
    cache_values,
    cache_len,
    out_weight,
    norm_gain,
    expert_ids,
    route_weights,
    w_gate,
    w_up,
    w_down,
):
    slot_count = lax.axis_size("seq")
    per_rows = queries.shape[0]
    members = slot_count // KVH
    group_q = QH // KVH
    new_count = per_rows * slot_count
    position_index = lax.axis_index("seq")
    member = position_index // KVH
    query_rows, key_new, value_new = (
        lax.all_to_all(queries, "seq", split_axis=1, concat_axis=0, tiled=True),
        lax.all_to_all(keys, "seq", split_axis=1, concat_axis=0, tiled=True),
        lax.all_to_all(values, "seq", split_axis=1, concat_axis=0, tiled=True),
    )
    key_rows = jnp.concatenate([cache_keys[0], key_new.reshape(new_count, HD)], axis=0)
    value_rows = jnp.concatenate([cache_values[0], value_new.reshape(new_count, HD)], axis=0)
    lengths = lax.dynamic_slice_in_dim(cache_len, member, 1, 1)[:, 0]
    attended = attend(query_rows.reshape(new_count, group_q, HD), key_rows, value_rows, lengths)
    returned_heads = lax.all_to_all(
        attended[:, None, :], "seq", split_axis=0, concat_axis=1, tiled=True
    )
    token_heads = returned_heads.reshape(per_rows * members, QH * HD)
    projected_f = jnp.dot(
        token_heads,
        lax.all_gather(out_weight, "seq", axis=0, tiled=True),
        preferred_element_type=jnp.float32,
    )
    projected_f = projected_f.reshape(per_rows, members, D)
    projected = projected_f.astype(jnp.bfloat16)
    token_count = per_rows * members
    flat_rows = projected.reshape(token_count, D).astype(jnp.float32)
    stats = jnp.mean(flat_rows * flat_rows, axis=-1, keepdims=True)
    normed = (flat_rows * lax.rsqrt(stats + 1e-06) * norm_gain.astype(jnp.float32)).astype(
        jnp.bfloat16
    )
    exp_dev = w_gate.shape[0]
    expert_count = exp_dev * slot_count
    chosen_ids = expert_ids.reshape(token_count * TOPK)
    onehot = (chosen_ids[:, None] == jnp.arange(expert_count, dtype=jnp.int32)[None, :]).astype(
        jnp.int32
    )
    slot_rank = jnp.sum((jnp.cumsum(onehot, axis=0) - onehot) * onehot, axis=1)
    owner = chosen_ids // exp_dev
    local_expert = chosen_ids % exp_dev
    slot_target = (local_expert * slot_count + owner) * CAP + slot_rank
    total_slots = exp_dev * slot_count * CAP
    token_of = jnp.arange(token_count * TOPK, dtype=jnp.int32) // TOPK
    source_row = jnp.full((total_slots,), -1, jnp.int32).at[slot_target].set(token_of)
    filled = source_row >= 0
    outgoing = jnp.where(
        filled[:, None], normed[jnp.maximum(source_row, 0)], jnp.zeros((), jnp.bfloat16)
    )
    outgoing = outgoing.reshape(exp_dev, slot_count, CAP, D)
    incoming = lax.all_to_all(outgoing, "seq", split_axis=1, concat_axis=1, tiled=True)
    row_block = incoming.reshape(exp_dev, slot_count * CAP, D)
    gate_out = jnp.einsum("ecd,edf->ecf", row_block, w_gate, preferred_element_type=jnp.float32)
    up_out = jnp.einsum("ecd,edf->ecf", row_block, w_up, preferred_element_type=jnp.float32)
    hidden_act = (jax.nn.silu(gate_out) * up_out).astype(jnp.bfloat16)
    expert_out = jnp.einsum(
        "ecf,efd->ecd", hidden_act, w_down, preferred_element_type=jnp.float32
    ).astype(jnp.bfloat16)
    expert_back = lax.all_to_all(
        expert_out.reshape(exp_dev, slot_count, CAP, D),
        "seq",
        split_axis=1,
        concat_axis=1,
        tiled=True,
    )
    picked = expert_back.reshape(total_slots, D)[slot_target].reshape(token_count, TOPK, D)
    raw_weights = route_weights.reshape(token_count, TOPK)
    norm_weights = raw_weights / jnp.sum(raw_weights, axis=1, keepdims=True)
    mixed = jnp.sum(norm_weights[:, :, None] * picked.astype(jnp.float32), axis=1)
    moe_out = mixed.astype(jnp.bfloat16).reshape(per_rows, members, D)
    return (projected, moe_out)


def solution(mesh):
    return jax.shard_map(
        body,
        mesh=mesh,
        in_specs=(
            P("seq", "groups", None),
            P("seq", "groups", None),
            P("seq", "groups", None),
            P(("groups", "seq"), None, None),
            P(("groups", "seq"), None, None),
            P(None, "groups"),
            P("seq", None),
            P(),
            P("seq", "groups", None),
            P("seq", "groups", None),
            P("seq", None, None),
            P("seq", None, None),
            P("seq", None, None),
        ),
        out_specs=(P("seq", "groups", None), P("seq", "groups", None)),
        check_vma=False,
    )
```

profile of v0, /device:TPU:0, one launch (start us, length us, event | category | flops | bytes accessed | tf_op | source)
XLA Modules:
  0.0 167.0 jit_solution(5124968312826070863)
XLA Ops:
  7.9 1.7 %copy.33 = bf16[2,16,1024]{2,0,1:T(2,128)(2,1)} copy(bf16[2,16,1024]{2,1,0:T(8,128)(2,1)} %param.13) | data formatting | bytes 131072 | tf_op args[0]
  9.7 7.4 %all-to-all-start.2 = ((bf16[2,16,1024]{2,0,1:T(2,128)(2,1)}), bf16[2,16,1024]{2,0,1:T(2,128)(2,1)S(1)}, u32[]{:S(2)}, u32[]{:S(2)}) async-start(bf16[2,16,1024]{2,0,1:T(2,128)(2,1)} %copy.33), calls=%async_computation.2 | async-start | bytes 131072 | tf_op jit(solution)/shard_map/all_to_all | solution.py:58
  17.1 0.8 eq.17
  17.9 0.8 reshape.224
  20.0 1.3 copy.32
  21.3 1.0 scatter_custom_fusion
  22.3 1.7 %all-to-all-done.2 = bf16[2,16,1024]{2,0,1:T(2,128)(2,1)S(1)} async-done(((bf16[2,16,1024]{2,0,1:T(2,128)(2,1)}), bf16[2,16,1024]{2,0,1:T(2,128)(2,1)S(1)}, u32[]{:S(2)}, u32[]{:S(2)}) %all-to-all-start.2) | async-done | bytes 65568 | tf_op jit(solution)/shard_map/all_to_all | solution.py:58
  24.0 4.3 %all-to-all-start.1 = ((bf16[2,16,128]{2,0,1:T(2,128)(2,1)}), bf16[2,16,128]{2,0,1:T(2,128)(2,1)S(1)}, u32[]{:S(2)}, u32[]{:S(2)}) async-start(bf16[2,16,128]{2,0,1:T(2,128)(2,1)} %copy.32), calls=%async_computation.1 | async-start | bytes 16384 | tf_op jit(solution)/shard_map/all_to_all | solution.py:59
  28.3 1.3 copy.31
  29.7 5.3 %all-to-all-done.1 = bf16[2,16,128]{2,0,1:T(2,128)(2,1)S(1)} async-done(((bf16[2,16,128]{2,0,1:T(2,128)(2,1)}), bf16[2,16,128]{2,0,1:T(2,128)(2,1)S(1)}, u32[]{:S(2)}, u32[]{:S(2)}) %all-to-all-start.1) | async-done | bytes 8224 | tf_op jit(solution)/shard_map/all_to_all | solution.py:59
  34.9 3.5 %all-to-all-start = ((bf16[2,16,128]{2,0,1:T(2,128)(2,1)}), bf16[2,16,128]{2,0,1:T(2,128)(2,1)S(1)}, u32[]{:S(2)}, u32[]{:S(2)}) async-start(bf16[2,16,128]{2,0,1:T(2,128)(2,1)} %copy.31), calls=%async_computation | async-start | bytes 16384 | tf_op jit(solution)/shard_map/all_to_all | solution.py:60
  38.4 3.4 %fusion.50 = (f32[8,32]{1,0:T(8,128)S(1)}, f32[8,32,2080]{2,1,0:T(8,128)}) fusion(pred[32,2080]{1,0:T(8,128)(4,1)S(1)} %pad_add_fusion, bf16[32,128]{1,0:T(8,128)(2,1)S(1)} %bitcast.89, bf16[2048,128]{1,0:T(8,128)(2,1)} %bitcast.91, bf16[32,8,128]{2,1,0:T(8,128)(2,1)S(1)} %reshape.222), kind=kOutput, calls=%fused_computation.81 | convolution fusion | flops 139511840 | bytes 2795520 | tf_op jit(solution)/shard_map/sub | solution.py:28
  41.8 2.9 %all-to-all-done = bf16[2,16,128]{2,0,1:T(2,128)(2,1)S(1)} async-done(((bf16[2,16,128]{2,0,1:T(2,128)(2,1)}), bf16[2,16,128]{2,0,1:T(2,128)(2,1)S(1)}, u32[]{:S(2)}, u32[]{:S(2)}) %all-to-all-start) | async-done | bytes 8224 | tf_op jit(solution)/shard_map/all_to_all | solution.py:60
  44.7 2.3 %fusion.11 = bf16[32,8,128]{2,0,1:T(8,128)(2,1)S(1)} fusion(f32[8,32,2080]{2,1,0:T(8,128)} %get-tuple-element.3, f32[8,32]{1,0:T(8,128)S(1)} %get-tuple-element.2, bf16[32,128]{1,0:T(8,128)(2,1)S(1)} %bitcast.90, bf16[2048,128]{1,0:T(8,128)(2,1)} %bitcast.92), kind=kOutput, calls=%fused_computation.17 | convolution fusion | flops 138477568 | bytes 2728960 | tf_op jit(solution)/shard_map/hqk,kd->qhd/dot_general | solution.py:31
  47.6 1.0 reduce.3
  49.3 3.5 %all-to-all-start.3 = ((bf16[16,2,1024]{2,1,0:T(2,128)(2,1)}), bf16[16,2,1024]{2,1,0:T(2,128)(2,1)S(1)}, u32[]{:S(2)}, u32[]{:S(2)}) async-start(bf16[16,2,1024]{2,1,0:T(2,128)(2,1)} %reshape.261), calls=%async_computation.3 | async-start | bytes 131072 | tf_op jit(solution)/shard_map/all_to_all | solution.py:66
  53.0 8.1 %all-to-all-done.3 = bf16[16,2,1024]{2,1,0:T(2,128)(2,1)S(1)} async-done(((bf16[16,2,1024]{2,1,0:T(2,128)(2,1)}), bf16[16,2,1024]{2,1,0:T(2,128)(2,1)S(1)}, u32[]{:S(2)}, u32[]{:S(2)}) %all-to-all-start.3) | async-done | bytes 65568 | tf_op jit(solution)/shard_map/all_to_all | solution.py:66
  61.6 26.4 %all-gather.2.cloned.1.call-done = bf16[2048,2048]{1,0:T(8,128)(2,1)} async-done(((bf16[128,2048]{1,0:T(8,128)(2,1)}), bf16[2048,2048]{1,0:T(8,128)(2,1)}) %all-gather.2.cloned.1.call-update) | async-done | bytes 8388624 | tf_op jit(solution)/shard_map/all_gather | solution.py:72
  88.0 4.7 %fusion.29 = (f32[2,8]{1,0:T(2,128)S(1)}, bf16[2,8,2048]{2,1,0:T(8,128)(2,1)S(1)}) fusion(bf16[2,8,2048]{2,1,0:T(8,128)(2,1)S(1)} %dot_general.22, bf16[2048,2048]{1,0:T(8,128)(2,1)} %all-gather.2.cloned.1.call-done), kind=kOutput, calls=%fused_computation.42 | convolution fusion | flops 134348784 | bytes 8519744 | tf_op jit(solution)/shard_map/dot_general | solution.py:70
  92.9 1.9 %gather_fusion = bf16[160,2048]{1,0:T(8,128)(2,1)} fusion(bf16[16,2048]{1,0:T(8,128)(2,1)S(1)} %fusion.28, s32[1024]{0:T(1024)S(1)} %pad_clamp_fusion.1), kind=kCustom, calls=%fused_computation | custom fusion | bytes 1311360 | tf_op jit(solution)/shard_map/gather | solution.py:98
  94.8 2.2 %gather.9 = bf16[2,16,5,2048]{3,2,1,0:T(8,128)(2,1)} reshape(bf16[160,2048]{1,0:T(8,128)(2,1)} %gather_fusion) | data formatting | bytes 1310720 | tf_op jit(solution)/shard_map/gather | solution.py:98
  97.0 1.5 broadcast_select_fusion
  99.3 21.4 %all_to_all.70 = bf16[2,16,5,2048]{3,0,2,1:T(2,128)(2,1)S(1)} all-to-all(bf16[2,16,5,2048]{3,0,2,1:T(2,128)(2,1)S(1)} %copy.40), channel_id=1, replica_groups=mesh['groups'=2,'seq'=16] {'seq'}, dimensions={1} | all-to-all | bytes 1310720 | tf_op jit(solution)/shard_map/all_to_all | solution.py:101
  120.7 0.9 copy-done.1
  122.3 4.3 %convolution_convert_fusion = bf16[2,80,2048]{2,1,0:T(8,128)(2,1)} fusion(bf16[2,384,2048]{2,1,0:T(8,128)(2,1)S(1)} %copy-done, bf16[2,2048,384]{2,1,0:T(8,128)(2,1)} %param.24, bf16[2,80,2048]{2,0,1:T(2,128)(2,1)} %bitcast.83, f32[2,80,384]{2,1,0:T(8,128)S(1)} %fusion.15), kind=kOutput, calls=%fused_computation.11 | convolution fusion | flops 504012800 | bytes 7847936 | tf_op jit(solution)/shard_map/ecf,efd->ecd/dot_general | solution.py:106
  126.6 2.6 %copy.43 = bf16[2,80,2048]{2,0,1:T(2,128)(2,1)} copy(bf16[2,80,2048]{2,1,0:T(8,128)(2,1)} %convolution_convert_fusion) | data formatting | bytes 1310720 | tf_op jit(solution)/shard_map/convert_element_type | solution.py:108
  129.2 4.3 %all-to-all-start.5 = ((bf16[2,16,5,2048]{3,0,2,1:T(2,128)(2,1)}), bf16[2,16,5,2048]{3,0,2,1:T(2,128)(2,1)}, u32[]{:S(2)}, u32[]{:S(2)}) async-start(bf16[2,16,5,2048]{3,0,2,1:T(2,128)(2,1)} %bitcast.84), calls=%async_computation.5 | async-start | bytes 1310720 | tf_op jit(solution)/shard_map/all_to_all | solution.py:109
  133.8 16.2 %all-to-all-done.5 = bf16[2,16,5,2048]{3,0,2,1:T(2,128)(2,1)} async-done(((bf16[2,16,5,2048]{3,0,2,1:T(2,128)(2,1)}), bf16[2,16,5,2048]{3,0,2,1:T(2,128)(2,1)}, u32[]{:S(2)}, u32[]{:S(2)}) %all-to-all-start.5) | async-done | bytes 655392 | tf_op jit(solution)/shard_map/all_to_all | solution.py:109
  150.1 2.4 %copy.44 = bf16[2,16,5,2048]{3,2,1,0:T(8,128)(2,1)} copy(bf16[2,16,5,2048]{3,0,2,1:T(2,128)(2,1)} %all-to-all-done.5) | data formatting | bytes 1310720 | tf_op jit(solution)/shard_map/all_to_all | solution.py:109
  152.4 2.2 %reshape.227 = bf16[160,2048]{1,0:T(8,128)(2,1)} reshape(bf16[2,16,5,2048]{3,2,1,0:T(8,128)(2,1)} %copy.44) | data formatting | bytes 1310720 | tf_op jit(solution)/shard_map/reshape | solution.py:116
  154.6 3.4 %gather_fusion.1 = bf16[128,2048]{1,0:T(8,128)(2,1)} fusion(bf16[160,2048]{1,0:T(8,128)(2,1)} %reshape.227, s32[1024]{0:T(1024)S(1)} %pad_clamp_fusion), kind=kCustom, calls=%fused_computation.1 | custom fusion | bytes 1049088 | tf_op jit(solution)/shard_map/gather | solution.py:116
  158.0 2.1 %fusion.12 = bf16[16,2048]{1,0:T(8,128)(2,1)} fusion(bf16[128,2048]{1,0:T(8,128)(2,1)} %gather_fusion.1, f32[16,8]{1,0:T(8,128)S(1)} %copy.39), kind=kLoop, calls=%fused_computation.19 | loop fusion | flops 753664 | bytes 590336 | tf_op jit(solution)/shard_map/reduce_sum | solution.py:119
  (48 shorter events, 5.9 us)
Async XLA Ops:
  7.2 115.2 %copy-start = (bf16[2,384,2048]{2,1,0:T(8,128)(2,1)S(1)}, bf16[2,384,2048]{2,1,0:T(8,128)(2,1)}, u32[]{:S(2)}) copy-start(bf16[2,384,2048]{2,1,0:T(8,128)(2,1)} %param.25) | copy-start | bytes 9437188
  7.2 80.9 %all-gather.2.cloned.1.call-start = ((), (), s32[]{:S(2)}) async-start(), calls=%async_computation.6 | async-start | bytes 8912896 | tf_op jit(solution)/shard_map/all_gather | solution.py:72
  9.7 14.3 %all-to-all-start.2 = ((bf16[2,16,1024]{2,0,1:T(2,128)(2,1)}), bf16[2,16,1024]{2,0,1:T(2,128)(2,1)S(1)}, u32[]{:S(2)}, u32[]{:S(2)}) async-start(bf16[2,16,1024]{2,0,1:T(2,128)(2,1)} %copy.33), calls=%async_computation.2 | async-start | bytes 131072 | tf_op jit(solution)/shard_map/all_to_all | solution.py:58
  24.0 10.9 %all-to-all-start.1 = ((bf16[2,16,128]{2,0,1:T(2,128)(2,1)}), bf16[2,16,128]{2,0,1:T(2,128)(2,1)S(1)}, u32[]{:S(2)}, u32[]{:S(2)}) async-start(bf16[2,16,128]{2,0,1:T(2,128)(2,1)} %copy.32), calls=%async_computation.1 | async-start | bytes 16384 | tf_op jit(solution)/shard_map/all_to_all | solution.py:59
  34.9 9.8 %all-to-all-start = ((bf16[2,16,128]{2,0,1:T(2,128)(2,1)}), bf16[2,16,128]{2,0,1:T(2,128)(2,1)S(1)}, u32[]{:S(2)}, u32[]{:S(2)}) async-start(bf16[2,16,128]{2,0,1:T(2,128)(2,1)} %copy.31), calls=%async_computation | async-start | bytes 16384 | tf_op jit(solution)/shard_map/all_to_all | solution.py:60
  44.7 8.1 %copy-start.5 = (bf16[2048]{0:T(1024)(128)(2,1)S(1)}, bf16[2048]{0:T(1024)(128)(2,1)}, u32[]{:S(2)}) copy-start(bf16[2048]{0:T(1024)(128)(2,1)} %param.20) | copy-start | bytes 12292
  49.3 11.8 %all-to-all-start.3 = ((bf16[16,2,1024]{2,1,0:T(2,128)(2,1)}), bf16[16,2,1024]{2,1,0:T(2,128)(2,1)S(1)}, u32[]{:S(2)}, u32[]{:S(2)}) async-start(bf16[16,2,1024]{2,1,0:T(2,128)(2,1)} %reshape.261), calls=%async_computation.3 | async-start | bytes 131072 | tf_op jit(solution)/shard_map/all_to_all | solution.py:66
  92.7 2.1 %copy-start.3 = (bf16[2,8,2048]{2,1,0:T(8,128)(2,1)}, bf16[2,8,2048]{2,1,0:T(8,128)(2,1)S(1)}, u32[]{:S(2)}) copy-start(bf16[2,8,2048]{2,1,0:T(8,128)(2,1)S(1)} %get-tuple-element.5) | copy-start | bytes 196612
  97.0 24.5 %copy-start.2 = (bf16[2,2048,384]{2,1,0:T(8,128)(2,1)S(1)}, bf16[2,2048,384]{2,1,0:T(8,128)(2,1)}, u32[]{:S(2)}) copy-start(bf16[2,2048,384]{2,1,0:T(8,128)(2,1)} %param.23) | copy-start | bytes 9437188
  120.7 0.9 copy-start.1
  126.6 6.9 %copy-start.4 = (f32[2,8,8]{2,1,0:T(8,128)S(1)}, f32[2,8,8]{2,1,0:T(8,128)}, u32[]{:S(2)}) copy-start(f32[2,8,8]{2,1,0:T(8,128)} %param.22) | copy-start | bytes 1540
  129.2 20.9 %all-to-all-start.5 = ((bf16[2,16,5,2048]{3,0,2,1:T(2,128)(2,1)}), bf16[2,16,5,2048]{3,0,2,1:T(2,128)(2,1)}, u32[]{:S(2)}, u32[]{:S(2)}) async-start(bf16[2,16,5,2048]{3,0,2,1:T(2,128)(2,1)} %bitcast.84), calls=%async_computation.5 | async-start | bytes 1310720 | tf_op jit(solution)/shard_map/all_to_all | solution.py:109
Sparse Core Ops, SparseCore 0:
  10.2 77.8 all-gather.1
where the time goes:
time: 168 us; the launch traced here: 167 us
  waiting for transfers between devices  61.4 us (37%)
  local copies, waits for them, and re-layouts  25.7 us (15%)
  starting transfers between devices  23 us (14%)
  blocking collectives  21.4 us (13%)
  matrix products  15.4 us (9%)
  between operations  14.3 us (9%)
  other arithmetic  5.82 us (3%)
    all_gather x1, waiting for transfers between devices, body(): lax.all_gather(out_weight, 'seq', axis=0, tiled=True)  26.4 us
    all_to_all x1, blocking collectives, body(): lax.all_to_all(outgoing, 'seq', split_axis=1, concat_axis=1, tiled=True)  21.4 us
    all_to_all x1, waiting for transfers between devices, body(): lax.all_to_all(expert_out.reshape(exp_dev, slot_count, CAP, D), 'seq', sp...  16.2 us
    all_to_all x1, waiting for transfers between devices, body(): lax.all_to_all(attended[:, None, :], 'seq', split_axis=0, concat_axis=1,...  8.13 us
    all_to_all x1, starting transfers between devices, body(): lax.all_to_all(queries, 'seq', split_axis=1, concat_axis=0, tiled=True)  7.41 us
    unnamed x17, local copies, waits for them, and re-layouts  5.94 us
    all_to_all x1, waiting for transfers between devices, body(): lax.all_to_all(keys, 'seq', split_axis=1, concat_axis=0, tiled=True)  5.26 us
    dot_general x1, matrix products, body(): jnp.dot(token_heads, lax.all_gather(out_weight, 'seq', axis=0, tiled=True...  4.66 us
  transfers between devices with their start and end apart: 6, of which 6 were waited for; matrix products, arithmetic and copies ran while one was open for 10% of the time, Pallas kernels for 0%

commit v1 on v0

--- a/solution.py
+++ b/solution.py
@@ -9,6 +9,17 @@
 QH = 16
 KVH = 2
 CAP = 5
+
+
+def cut_along(x, dim, size):
+    before, after = (x.shape[:dim], x.shape[dim + 1 :])
+    return jnp.moveaxis(x.reshape(*before, size, -1, *after), dim, 0)
+
+
+def in_order(blocks, dim):
+    blocks = jnp.moveaxis(blocks, 0, dim)
+    lengths = blocks.shape
+    return blocks.reshape(*lengths[:dim], lengths[dim] * lengths[dim + 1], *lengths[dim + 2 :])
 
 
 def attend(query_heads, key_rows, value_rows, lengths):
@@ -63,9 +74,15 @@
     value_rows = jnp.concatenate([cache_values[0], value_new.reshape(new_count, HD)], axis=0)
     lengths = lax.dynamic_slice_in_dim(cache_len, member, 1, 1)[:, 0]
     attended = attend(query_rows.reshape(new_count, group_q, HD), key_rows, value_rows, lengths)
-    returned_heads = lax.all_to_all(
-        attended[:, None, :], "seq", split_axis=0, concat_axis=1, tiled=True
-    )
+    array = attended[:, None, :]
+    length, index = (lax.axis_size("seq"), lax.axis_index("seq"))
+    blocks = cut_along(array, 0, length)
+    finished = [blocks[index]]
+    for step in range(1, length):
+        sent = blocks[index ^ step]
+        finished.append(lax.ppermute(sent, "seq", [(i, i ^ step) for i in range(length)]))
+    blocks = jnp.stack(finished)[index ^ jnp.arange(length)]
+    returned_heads = in_order(blocks, 1)
     token_heads = returned_heads.reshape(per_rows * members, QH * HD)
     projected_f = jnp.dot(
         token_heads,

time: 168 us -> 168 us (level)
  starting transfers between devices: 23 us -> 40.6 us
  waiting for transfers between devices: 61.4 us -> 45.4 us
    ppermute x0 -> x15, starting transfers between devices: none -> 21.1 us  [body(): lax.ppermute(sent, 'seq', [(i, i ^ step) for i in range(length)])]
    all_gather x1, waiting for transfers between devices: 26.4 us -> 15.6 us  [body(): lax.all_gather(out_weight, 'seq', axis=0, tiled=True)]
    all_to_all x1 -> x0, waiting for transfers between devices: 8.13 us -> none  [body(): lax.all_to_all(attended[:, None, :], 'seq', split_axis=0, concat_axis=1,...]
    all_to_all x1 -> x0, starting transfers between devices: 3.5 us -> none  [body(): lax.all_to_all(attended[:, None, :], 'seq', split_axis=0, concat_axis=1,...]
    ppermute x0 -> x15, waiting for transfers between devices: none -> 3.15 us  [body(): lax.ppermute(sent, 'seq', [(i, i ^ step) for i in range(length)])]
    unnamed x17 -> x29, local copies, waits for them, and re-layouts: 5.94 us -> 5.4 us
  transfers between devices with their start and end apart: 6 -> 20, of which waited for: 6 -> 7; matrix products, arithmetic and copies ran while one was open for 10% -> 9% of each run, Pallas kernels for 0% -> 0%
where the time goes in v1:
time: 168 us; the launch traced here: 167 us
  waiting for transfers between devices  45.4 us (27%)
  starting transfers between devices  40.6 us (24%)
  local copies, waits for them, and re-layouts  25.5 us (15%)
  blocking collectives  21.3 us (13%)
  matrix products  15.4 us (9%)
  between operations  14.4 us (9%)
  other arithmetic  4.46 us (3%)
    all_to_all x1, blocking collectives, body(): lax.all_to_all(outgoing, 'seq', split_axis=1, concat_axis=1, tiled=True)  21.3 us
    ppermute x15, starting transfers between devices, body(): lax.ppermute(sent, 'seq', [(i, i ^ step) for i in range(length)])  21.1 us
    all_to_all x1, waiting for transfers between devices, body(): lax.all_to_all(expert_out.reshape(exp_dev, slot_count, CAP, D), 'seq', sp...  16.2 us
    all_gather x1, waiting for transfers between devices, body(): lax.all_gather(out_weight, 'seq', axis=0, tiled=True)  15.6 us
    all_to_all x1, starting transfers between devices, body(): lax.all_to_all(queries, 'seq', split_axis=1, concat_axis=0, tiled=True)  7.41 us
    unnamed x29, local copies, waits for them, and re-layouts  5.4 us
    all_to_all x1, waiting for transfers between devices, body(): lax.all_to_all(keys, 'seq', split_axis=1, concat_axis=0, tiled=True)  5.19 us
    dot_general x1, matrix products, body(): jnp.dot(token_heads, lax.all_gather(out_weight, 'seq', axis=0, tiled=True...  4.66 us
  transfers between devices with their start and end apart: 20, of which 7 were waited for; matrix products, arithmetic and copies ran while one was open for 9% of the time, Pallas kernels for 0%

profile of v1, /device:TPU:0, one launch (start us, length us, event | category | flops | bytes accessed | tf_op | source)
XLA Modules:
  0.0 167.2 jit_solution(11830878689470445380)
XLA Ops:
  7.9 1.7 %copy.79 = bf16[2,16,1024]{2,0,1:T(2,128)(2,1)} copy(bf16[2,16,1024]{2,1,0:T(8,128)(2,1)} %param.13) | data formatting | bytes 131072 | tf_op args[0]
  9.7 7.4 %all-to-all-start.2 = ((bf16[2,16,1024]{2,0,1:T(2,128)(2,1)}), bf16[2,16,1024]{2,0,1:T(2,128)(2,1)S(1)}, u32[]{:S(2)}, u32[]{:S(2)}) async-start(bf16[2,16,1024]{2,0,1:T(2,128)(2,1)} %copy.79), calls=%async_computation.2 | async-start | bytes 131072 | tf_op jit(solution)/shard_map/all_to_all | solution.py:69
  21.0 1.3 copy.78
  22.3 1.7 %all-to-all-done.2 = bf16[2,16,1024]{2,0,1:T(2,128)(2,1)S(1)} async-done(((bf16[2,16,1024]{2,0,1:T(2,128)(2,1)}), bf16[2,16,1024]{2,0,1:T(2,128)(2,1)S(1)}, u32[]{:S(2)}, u32[]{:S(2)}) %all-to-all-start.2) | async-done | bytes 65568 | tf_op jit(solution)/shard_map/all_to_all | solution.py:69
  24.0 4.3 %all-to-all-start.1 = ((bf16[2,16,128]{2,0,1:T(2,128)(2,1)}), bf16[2,16,128]{2,0,1:T(2,128)(2,1)S(1)}, u32[]{:S(2)}, u32[]{:S(2)}) async-start(bf16[2,16,128]{2,0,1:T(2,128)(2,1)} %copy.78), calls=%async_computation.1 | async-start | bytes 16384 | tf_op jit(solution)/shard_map/all_to_all | solution.py:70
  29.8 5.2 %all-to-all-done.1 = bf16[2,16,128]{2,0,1:T(2,128)(2,1)S(1)} async-done(((bf16[2,16,128]{2,0,1:T(2,128)(2,1)}), bf16[2,16,128]{2,0,1:T(2,128)(2,1)S(1)}, u32[]{:S(2)}, u32[]{:S(2)}) %all-to-all-start.1) | async-done | bytes 8224 | tf_op jit(solution)/shard_map/all_to_all | solution.py:70
  34.9 3.5 %all-to-all-start = ((bf16[2,16,128]{2,0,1:T(2,128)(2,1)}), bf16[2,16,128]{2,0,1:T(2,128)(2,1)S(1)}, u32[]{:S(2)}, u32[]{:S(2)}) async-start(bf16[2,16,128]{2,0,1:T(2,128)(2,1)} %copy.77), calls=%async_computation | async-start | bytes 16384 | tf_op jit(solution)/shard_map/all_to_all | solution.py:71
  38.4 3.4 %fusion.67 = (f32[8,32]{1,0:T(8,128)S(1)}, f32[8,32,2080]{2,1,0:T(8,128)}) fusion(pred[32,2080]{1,0:T(8,128)(4,1)S(1)} %pad_add_fusion, bf16[32,128]{1,0:T(8,128)(2,1)S(1)} %bitcast.185, bf16[2048,128]{1,0:T(8,128)(2,1)} %bitcast.187, bf16[32,8,128]{2,1,0:T(8,128)(2,1)S(1)} %reshape.236), kind=kOutput, calls=%fused_computation.133 | convolution fusion | flops 139511840 | bytes 2795520 | tf_op jit(solution)/shard_map/sub | solution.py:39
  41.8 2.9 %all-to-all-done = bf16[2,16,128]{2,0,1:T(2,128)(2,1)S(1)} async-done(((bf16[2,16,128]{2,0,1:T(2,128)(2,1)}), bf16[2,16,128]{2,0,1:T(2,128)(2,1)S(1)}, u32[]{:S(2)}, u32[]{:S(2)}) %all-to-all-start) | async-done | bytes 8224 | tf_op jit(solution)/shard_map/all_to_all | solution.py:71
  44.7 2.3 %fusion.11 = bf16[32,8,128]{2,0,1:T(8,128)(2,1)S(1)} fusion(f32[8,32,2080]{2,1,0:T(8,128)} %get-tuple-element.19, f32[8,32]{1,0:T(8,128)S(1)} %get-tuple-element.18, bf16[32,128]{1,0:T(8,128)(2,1)S(1)} %bitcast.186, bf16[2048,128]{1,0:T(8,128)(2,1)} %bitcast.188), kind=kOutput, calls=%fused_computation.18 | convolution fusion | flops 138477568 | bytes 2728960 | tf_op jit(solution)/shard_map/hqk,kd->qhd/dot_general | solution.py:42
  48.0 1.3 collective-permute-start.2
  51.6 2.3 %collective-permute-start.6 = (bf16[2,1,1024]{2,0,1:T(2,128)(2,1)S(1)}, bf16[2,1,1024]{2,0,1:T(2,128)(2,1)S(1)}, u32[]{:S(2)}, u32[]{:S(2)}) collective-permute-start(bf16[2,1,1024]{2,0,1:T(2,128)(2,1)S(1)} %get-tuple-element.10), channel_id=1, source_target_pairs={{0,7},{1,6},{2,5},{3,4},{4,3},{5,2},{6,1},{7,0},{8,15},{9,14},{10,... | collective-permute-start | bytes 12296 | tf_op jit(solution)/shard_map/ppermute | solution.py:83
  54.5 2.1 %collective-permute-start.8 = (bf16[2,1,1024]{2,0,1:T(2,128)(2,1)S(1)}, bf16[2,1,1024]{2,0,1:T(2,128)(2,1)S(1)}, u32[]{:S(2)}, u32[]{:S(2)}) collective-permute-start(bf16[2,1,1024]{2,0,1:T(2,128)(2,1)S(1)} %get-tuple-element.8), channel_id=1, source_target_pairs={{0,9},{1,8},{2,11},{3,10},{4,13},{5,12},{6,15},{7,14},{8,1},{9,0},... | collective-permute-start | bytes 12296 | tf_op jit(solution)/shard_map/ppermute | solution.py:83
  57.5 2.8 %collective-permute-start.10 = (bf16[2,1,1024]{2,0,1:T(2,128)(2,1)S(1)}, bf16[2,1,1024]{2,0,1:T(2,128)(2,1)S(1)}, u32[]{:S(2)}, u32[]{:S(2)}) collective-permute-start(bf16[2,1,1024]{2,0,1:T(2,128)(2,1)S(1)} %get-tuple-element.6), channel_id=1, source_target_pairs={{0,11},{1,10},{2,9},{3,8},{4,15},{5,14},{6,13},{7,12},{8,3},{9,2},... | collective-permute-start | bytes 12296 | tf_op jit(solution)/shard_map/ppermute | solution.py:83
  61.2 2.7 %collective-permute-start.12 = (bf16[2,1,1024]{2,0,1:T(2,128)(2,1)S(1)}, bf16[2,1,1024]{2,0,1:T(2,128)(2,1)S(1)}, u32[]{:S(2)}, u32[]{:S(2)}) collective-permute-start(bf16[2,1,1024]{2,0,1:T(2,128)(2,1)S(1)} %get-tuple-element.4), channel_id=1, source_target_pairs={{0,13},{1,12},{2,15},{3,14},{4,9},{5,8},{6,11},{7,10},{8,5},{9,4},... | collective-permute-start | bytes 12296 | tf_op jit(solution)/shard_map/ppermute | solution.py:83
  64.0 1.9 %collective-permute-start.13 = (bf16[2,1,1024]{2,0,1:T(2,128)(2,1)S(1)}, bf16[2,1,1024]{2,0,1:T(2,128)(2,1)S(1)}, u32[]{:S(2)}, u32[]{:S(2)}) collective-permute-start(bf16[2,1,1024]{2,0,1:T(2,128)(2,1)S(1)} %get-tuple-element.3), channel_id=1, source_target_pairs={{0,14},{1,15},{2,12},{3,13},{4,10},{5,11},{6,8},{7,9},{8,6},{9,7},... | collective-permute-start | bytes 12296 | tf_op jit(solution)/shard_map/ppermute | solution.py:83
  65.9 2.8 %collective-permute-start.14 = (bf16[2,1,1024]{2,0,1:T(2,128)(2,1)S(1)}, bf16[2,1,1024]{2,0,1:T(2,128)(2,1)S(1)}, u32[]{:S(2)}, u32[]{:S(2)}) collective-permute-start(bf16[2,1,1024]{2,0,1:T(2,128)(2,1)S(1)} %get-tuple-element.2), channel_id=1, source_target_pairs={{0,15},{1,14},{2,13},{3,12},{4,11},{5,10},{6,9},{7,8},{8,7},{9,6},... | collective-permute-start | bytes 12296 | tf_op jit(solution)/shard_map/ppermute | solution.py:83
  68.7 1.8 %collective-permute-done.13 = bf16[2,1,1024]{2,0,1:T(2,128)(2,1)S(1)} collective-permute-done((bf16[2,1,1024]{2,0,1:T(2,128)(2,1)S(1)}, bf16[2,1,1024]{2,0,1:T(2,128)(2,1)S(1)}, u32[]{:S(2)}, u32[]{:S(2)}) %collective-permute-start.13) | collective-permute-done | bytes 4128 | tf_op jit(solution)/shard_map/ppermute | solution.py:83
  72.6 15.6 %all-gather.2.cloned.1.call-done = bf16[2048,2048]{1,0:T(8,128)(2,1)} async-done(((bf16[128,2048]{1,0:T(8,128)(2,1)}), bf16[2048,2048]{1,0:T(8,128)(2,1)}) %all-gather.2.cloned.1.call-update) | async-done | bytes 8388624 | tf_op jit(solution)/shard_map/all_gather | solution.py:89
  88.2 4.7 %fusion.29 = (f32[2,8]{1,0:T(2,128)S(1)}, bf16[2,8,2048]{2,1,0:T(8,128)(2,1)S(1)}) fusion(bf16[2,8,2048]{2,1,0:T(8,128)(2,1)S(1)} %dot_general.22, bf16[2048,2048]{1,0:T(8,128)(2,1)} %all-gather.2.cloned.1.call-done), kind=kOutput, calls=%fused_computation.43 | convolution fusion | flops 134348784 | bytes 8519744 | tf_op jit(solution)/shard_map/dot_general | solution.py:87
  93.1 1.9 %gather_fusion.1 = bf16[160,2048]{1,0:T(8,128)(2,1)} fusion(bf16[16,2048]{1,0:T(8,128)(2,1)S(1)} %fusion.28, s32[1024]{0:T(1024)S(1)} %pad_clamp_fusion.1), kind=kCustom, calls=%fused_computation.1 | custom fusion | bytes 1311360 | tf_op jit(solution)/shard_map/gather | solution.py:115
  95.0 2.2 %gather.13 = bf16[2,16,5,2048]{3,2,1,0:T(8,128)(2,1)} reshape(bf16[160,2048]{1,0:T(8,128)(2,1)} %gather_fusion.1) | data formatting | bytes 1310720 | tf_op jit(solution)/shard_map/gather | solution.py:115
  97.2 1.5 broadcast_select_fusion
  99.5 21.3 %all_to_all.55 = bf16[2,16,5,2048]{3,0,2,1:T(2,128)(2,1)S(1)} all-to-all(bf16[2,16,5,2048]{3,0,2,1:T(2,128)(2,1)S(1)} %copy.102), channel_id=1, replica_groups=mesh['groups'=2,'seq'=16] {'seq'}, dimensions={1} | all-to-all | bytes 1310720 | tf_op jit(solution)/shard_map/all_to_all | solution.py:118
  122.5 4.3 %convolution_convert_fusion = bf16[2,80,2048]{2,1,0:T(8,128)(2,1)} fusion(bf16[2,384,2048]{2,1,0:T(8,128)(2,1)S(1)} %copy-done, bf16[2,2048,384]{2,1,0:T(8,128)(2,1)} %param.24, bf16[2,80,2048]{2,0,1:T(2,128)(2,1)} %bitcast.178, f32[2,80,384]{2,1,0:T(8,128)S(1)} %fusion.15), kind=kOutput, calls=%fused_computation.12 | convolution fusion | flops 504012800 | bytes 7847936 | tf_op jit(solution)/shard_map/ecf,efd->ecd/dot_general | solution.py:123
  126.8 2.6 %copy.105 = bf16[2,80,2048]{2,0,1:T(2,128)(2,1)} copy(bf16[2,80,2048]{2,1,0:T(8,128)(2,1)} %convolution_convert_fusion) | data formatting | bytes 1310720 | tf_op jit(solution)/shard_map/convert_element_type | solution.py:125
  129.4 4.3 %all-to-all-start.4 = ((bf16[2,16,5,2048]{3,0,2,1:T(2,128)(2,1)}), bf16[2,16,5,2048]{3,0,2,1:T(2,128)(2,1)}, u32[]{:S(2)}, u32[]{:S(2)}) async-start(bf16[2,16,5,2048]{3,0,2,1:T(2,128)(2,1)} %bitcast.179), calls=%async_computation.4 | async-start | bytes 1310720 | tf_op jit(solution)/shard_map/all_to_all | solution.py:126
  134.0 16.2 %all-to-all-done.4 = bf16[2,16,5,2048]{3,0,2,1:T(2,128)(2,1)} async-done(((bf16[2,16,5,2048]{3,0,2,1:T(2,128)(2,1)}), bf16[2,16,5,2048]{3,0,2,1:T(2,128)(2,1)}, u32[]{:S(2)}, u32[]{:S(2)}) %all-to-all-start.4) | async-done | bytes 655392 | tf_op jit(solution)/shard_map/all_to_all | solution.py:126
  150.2 2.4 %copy.106 = bf16[2,16,5,2048]{3,2,1,0:T(8,128)(2,1)} copy(bf16[2,16,5,2048]{3,0,2,1:T(2,128)(2,1)} %all-to-all-done.4) | data formatting | bytes 1310720 | tf_op jit(solution)/shard_map/all_to_all | solution.py:126
  152.6 2.2 %reshape.241 = bf16[160,2048]{1,0:T(8,128)(2,1)} reshape(bf16[2,16,5,2048]{3,2,1,0:T(8,128)(2,1)} %copy.106) | data formatting | bytes 1310720 | tf_op jit(solution)/shard_map/reshape | solution.py:133
  154.8 3.4 %gather_fusion.2 = bf16[128,2048]{1,0:T(8,128)(2,1)} fusion(bf16[160,2048]{1,0:T(8,128)(2,1)} %reshape.241, s32[1024]{0:T(1024)S(1)} %pad_clamp_fusion), kind=kCustom, calls=%fused_computation.2 | custom fusion | bytes 1049088 | tf_op jit(solution)/shard_map/gather | solution.py:133
  158.2 2.1 %fusion.12 = bf16[16,2048]{1,0:T(8,128)(2,1)} fusion(bf16[128,2048]{1,0:T(8,128)(2,1)} %gather_fusion.2, f32[16,8]{1,0:T(8,128)S(1)} %copy.101), kind=kLoop, calls=%fused_computation.20 | loop fusion | flops 753664 | bytes 590336 | tf_op jit(solution)/shard_map/reduce_sum | solution.py:136
  (89 shorter events, 16.5 us)
Async XLA Ops:
  7.2 115.3 %copy-start = (bf16[2,384,2048]{2,1,0:T(8,128)(2,1)S(1)}, bf16[2,384,2048]{2,1,0:T(8,128)(2,1)}, u32[]{:S(2)}) copy-start(bf16[2,384,2048]{2,1,0:T(8,128)(2,1)} %param.25) | copy-start | bytes 9437188
  7.2 81.1 %all-gather.2.cloned.1.call-start = ((), (), s32[]{:S(2)}) async-start(), calls=%async_computation.5 | async-start | bytes 8912896 | tf_op jit(solution)/shard_map/all_gather | solution.py:89
  9.7 14.3 %all-to-all-start.2 = ((bf16[2,16,1024]{2,0,1:T(2,128)(2,1)}), bf16[2,16,1024]{2,0,1:T(2,128)(2,1)S(1)}, u32[]{:S(2)}, u32[]{:S(2)}) async-start(bf16[2,16,1024]{2,0,1:T(2,128)(2,1)} %copy.79), calls=%async_computation.2 | async-start | bytes 131072 | tf_op jit(solution)/shard_map/all_to_all | solution.py:69
  24.0 11.0 %all-to-all-start.1 = ((bf16[2,16,128]{2,0,1:T(2,128)(2,1)}), bf16[2,16,128]{2,0,1:T(2,128)(2,1)S(1)}, u32[]{:S(2)}, u32[]{:S(2)}) async-start(bf16[2,16,128]{2,0,1:T(2,128)(2,1)} %copy.78), calls=%async_computation.1 | async-start | bytes 16384 | tf_op jit(solution)/shard_map/all_to_all | solution.py:70
  34.9 9.8 %all-to-all-start = ((bf16[2,16,128]{2,0,1:T(2,128)(2,1)}), bf16[2,16,128]{2,0,1:T(2,128)(2,1)S(1)}, u32[]{:S(2)}, u32[]{:S(2)}) async-start(bf16[2,16,128]{2,0,1:T(2,128)(2,1)} %copy.77), calls=%async_computation | async-start | bytes 16384 | tf_op jit(solution)/shard_map/all_to_all | solution.py:71
  44.7 2.6 %copy-start.5 = (bf16[2048]{0:T(1024)(128)(2,1)S(1)}, bf16[2048]{0:T(1024)(128)(2,1)}, u32[]{:S(2)}) copy-start(bf16[2048]{0:T(1024)(128)(2,1)} %param.20) | copy-start | bytes 12292
  47.3 3.8 %collective-permute-start = (bf16[2,1,1024]{2,0,1:T(2,128)(2,1)S(1)}, bf16[2,1,1024]{2,0,1:T(2,128)(2,1)S(1)}, u32[]{:S(2)}, u32[]{:S(2)}) collective-permute-start(bf16[2,1,1024]{2,0,1:T(2,128)(2,1)S(1)} %get-tuple-element.16), channel_id=1, source_target_pairs={{0,1},{1,0},{2,3},{3,2},{4,5},{5,4},{6,7},{7,6},{8,9},{9,8},{10,11... | collective-permute-start | bytes 12296 | tf_op jit(solution)/shard_map/ppermute | solution.py:83
  47.5 4.1 %collective-permute-start.1 = (bf16[2,1,1024]{2,0,1:T(2,128)(2,1)S(1)}, bf16[2,1,1024]{2,0,1:T(2,128)(2,1)S(1)}, u32[]{:S(2)}, u32[]{:S(2)}) collective-permute-start(bf16[2,1,1024]{2,0,1:T(2,128)(2,1)S(1)} %get-tuple-element.15), channel_id=1, source_target_pairs={{0,2},{1,3},{2,0},{3,1},{4,6},{5,7},{6,4},{7,5},{8,10},{9,11},{10,... | collective-permute-start | bytes 12296 | tf_op jit(solution)/shard_map/ppermute | solution.py:83
  48.0 5.8 %collective-permute-start.2 = (bf16[2,1,1024]{2,0,1:T(2,128)(2,1)S(1)}, bf16[2,1,1024]{2,0,1:T(2,128)(2,1)S(1)}, u32[]{:S(2)}, u32[]{:S(2)}) collective-permute-start(bf16[2,1,1024]{2,0,1:T(2,128)(2,1)S(1)} %get-tuple-element.14), channel_id=1, source_target_pairs={{0,3},{1,2},{2,1},{3,0},{4,7},{5,6},{6,5},{7,4},{8,11},{9,10},{10,... | collective-permute-start | bytes 12296 | tf_op jit(solution)/shard_map/ppermute | solution.py:83
  49.4 5.1 %collective-permute-start.3 = (bf16[2,1,1024]{2,0,1:T(2,128)(2,1)S(1)}, bf16[2,1,1024]{2,0,1:T(2,128)(2,1)S(1)}, u32[]{:S(2)}, u32[]{:S(2)}) collective-permute-start(bf16[2,1,1024]{2,0,1:T(2,128)(2,1)S(1)} %get-tuple-element.13), channel_id=1, source_target_pairs={{0,4},{1,5},{2,6},{3,7},{4,0},{5,1},{6,2},{7,3},{8,12},{9,13},{10,... | collective-permute-start | bytes 12296 | tf_op jit(solution)/shard_map/ppermute | solution.py:83
  49.9 6.7 %collective-permute-start.4 = (bf16[2,1,1024]{2,0,1:T(2,128)(2,1)S(1)}, bf16[2,1,1024]{2,0,1:T(2,128)(2,1)S(1)}, u32[]{:S(2)}, u32[]{:S(2)}) collective-permute-start(bf16[2,1,1024]{2,0,1:T(2,128)(2,1)S(1)} %get-tuple-element.12), channel_id=1, source_target_pairs={{0,5},{1,4},{2,7},{3,6},{4,1},{5,0},{6,3},{7,2},{8,13},{9,12},{10,... | collective-permute-start | bytes 12296 | tf_op jit(solution)/shard_map/ppermute | solution.py:83
  51.0 6.5 %collective-permute-start.5 = (bf16[2,1,1024]{2,0,1:T(2,128)(2,1)S(1)}, bf16[2,1,1024]{2,0,1:T(2,128)(2,1)S(1)}, u32[]{:S(2)}, u32[]{:S(2)}) collective-permute-start(bf16[2,1,1024]{2,0,1:T(2,128)(2,1)S(1)} %get-tuple-element.11), channel_id=1, source_target_pairs={{0,6},{1,7},{2,4},{3,5},{4,2},{5,3},{6,0},{7,1},{8,14},{9,15},{10,... | collective-permute-start | bytes 12296 | tf_op jit(solution)/shard_map/ppermute | solution.py:83
  51.6 8.8 %collective-permute-start.6 = (bf16[2,1,1024]{2,0,1:T(2,128)(2,1)S(1)}, bf16[2,1,1024]{2,0,1:T(2,128)(2,1)S(1)}, u32[]{:S(2)}, u32[]{:S(2)}) collective-permute-start(bf16[2,1,1024]{2,0,1:T(2,128)(2,1)S(1)} %get-tuple-element.10), channel_id=1, source_target_pairs={{0,7},{1,6},{2,5},{3,4},{4,3},{5,2},{6,1},{7,0},{8,15},{9,14},{10,... | collective-permute-start | bytes 12296 | tf_op jit(solution)/shard_map/ppermute | solution.py:83
  53.9 7.4 %collective-permute-start.7 = (bf16[2,1,1024]{2,0,1:T(2,128)(2,1)S(1)}, bf16[2,1,1024]{2,0,1:T(2,128)(2,1)S(1)}, u32[]{:S(2)}, u32[]{:S(2)}) collective-permute-start(bf16[2,1,1024]{2,0,1:T(2,128)(2,1)S(1)} %get-tuple-element.9), channel_id=1, source_target_pairs={{0,8},{1,9},{2,10},{3,11},{4,12},{5,13},{6,14},{7,15},{8,0},{9,1},... | collective-permute-start | bytes 12296 | tf_op jit(solution)/shard_map/ppermute | solution.py:83
  54.5 9.5 %collective-permute-start.8 = (bf16[2,1,1024]{2,0,1:T(2,128)(2,1)S(1)}, bf16[2,1,1024]{2,0,1:T(2,128)(2,1)S(1)}, u32[]{:S(2)}, u32[]{:S(2)}) collective-permute-start(bf16[2,1,1024]{2,0,1:T(2,128)(2,1)S(1)} %get-tuple-element.8), channel_id=1, source_target_pairs={{0,9},{1,8},{2,11},{3,10},{4,13},{5,12},{6,15},{7,14},{8,1},{9,0},... | collective-permute-start | bytes 12296 | tf_op jit(solution)/shard_map/ppermute | solution.py:83
  56.6 9.3 %collective-permute-start.9 = (bf16[2,1,1024]{2,0,1:T(2,128)(2,1)S(1)}, bf16[2,1,1024]{2,0,1:T(2,128)(2,1)S(1)}, u32[]{:S(2)}, u32[]{:S(2)}) collective-permute-start(bf16[2,1,1024]{2,0,1:T(2,128)(2,1)S(1)} %get-tuple-element.7), channel_id=1, source_target_pairs={{0,10},{1,11},{2,8},{3,9},{4,14},{5,15},{6,12},{7,13},{8,2},{9,3},... | collective-permute-start | bytes 12296 | tf_op jit(solution)/shard_map/ppermute | solution.py:83
  57.5 11.2 %collective-permute-start.10 = (bf16[2,1,1024]{2,0,1:T(2,128)(2,1)S(1)}, bf16[2,1,1024]{2,0,1:T(2,128)(2,1)S(1)}, u32[]{:S(2)}, u32[]{:S(2)}) collective-permute-start(bf16[2,1,1024]{2,0,1:T(2,128)(2,1)S(1)} %get-tuple-element.6), channel_id=1, source_target_pairs={{0,11},{1,10},{2,9},{3,8},{4,15},{5,14},{6,13},{7,12},{8,3},{9,2},... | collective-permute-start | bytes 12296 | tf_op jit(solution)/shard_map/ppermute | solution.py:83
  60.4 8.3 %collective-permute-start.11 = (bf16[2,1,1024]{2,0,1:T(2,128)(2,1)S(1)}, bf16[2,1,1024]{2,0,1:T(2,128)(2,1)S(1)}, u32[]{:S(2)}, u32[]{:S(2)}) collective-permute-start(bf16[2,1,1024]{2,0,1:T(2,128)(2,1)S(1)} %get-tuple-element.5), channel_id=1, source_target_pairs={{0,12},{1,13},{2,14},{3,15},{4,8},{5,9},{6,10},{7,11},{8,4},{9,5},... | collective-permute-start | bytes 12296 | tf_op jit(solution)/shard_map/ppermute | solution.py:83
  61.2 7.5 %collective-permute-start.12 = (bf16[2,1,1024]{2,0,1:T(2,128)(2,1)S(1)}, bf16[2,1,1024]{2,0,1:T(2,128)(2,1)S(1)}, u32[]{:S(2)}, u32[]{:S(2)}) collective-permute-start(bf16[2,1,1024]{2,0,1:T(2,128)(2,1)S(1)} %get-tuple-element.4), channel_id=1, source_target_pairs={{0,13},{1,12},{2,15},{3,14},{4,9},{5,8},{6,11},{7,10},{8,5},{9,4},... | collective-permute-start | bytes 12296 | tf_op jit(solution)/shard_map/ppermute | solution.py:83
  64.0 6.6 %collective-permute-start.13 = (bf16[2,1,1024]{2,0,1:T(2,128)(2,1)S(1)}, bf16[2,1,1024]{2,0,1:T(2,128)(2,1)S(1)}, u32[]{:S(2)}, u32[]{:S(2)}) collective-permute-start(bf16[2,1,1024]{2,0,1:T(2,128)(2,1)S(1)} %get-tuple-element.3), channel_id=1, source_target_pairs={{0,14},{1,15},{2,12},{3,13},{4,10},{5,11},{6,8},{7,9},{8,6},{9,7},... | collective-permute-start | bytes 12296 | tf_op jit(solution)/shard_map/ppermute | solution.py:83
  65.9 6.0 %collective-permute-start.14 = (bf16[2,1,1024]{2,0,1:T(2,128)(2,1)S(1)}, bf16[2,1,1024]{2,0,1:T(2,128)(2,1)S(1)}, u32[]{:S(2)}, u32[]{:S(2)}) collective-permute-start(bf16[2,1,1024]{2,0,1:T(2,128)(2,1)S(1)} %get-tuple-element.2), channel_id=1, source_target_pairs={{0,15},{1,14},{2,13},{3,12},{4,11},{5,10},{6,9},{7,8},{8,7},{9,6},... | collective-permute-start | bytes 12296 | tf_op jit(solution)/shard_map/ppermute | solution.py:83
  92.9 2.1 %copy-start.3 = (bf16[2,8,2048]{2,1,0:T(8,128)(2,1)}, bf16[2,8,2048]{2,1,0:T(8,128)(2,1)S(1)}, u32[]{:S(2)}) copy-start(bf16[2,8,2048]{2,1,0:T(8,128)(2,1)S(1)} %get-tuple-element.21) | copy-start | bytes 196612
  97.2 24.5 %copy-start.2 = (bf16[2,2048,384]{2,1,0:T(8,128)(2,1)S(1)}, bf16[2,2048,384]{2,1,0:T(8,128)(2,1)}, u32[]{:S(2)}) copy-start(bf16[2,2048,384]{2,1,0:T(8,128)(2,1)} %param.23) | copy-start | bytes 9437188
  120.8 0.9 copy-start.1
  126.8 6.9 %copy-start.4 = (f32[2,8,8]{2,1,0:T(8,128)S(1)}, f32[2,8,8]{2,1,0:T(8,128)}, u32[]{:S(2)}) copy-start(f32[2,8,8]{2,1,0:T(8,128)} %param.22) | copy-start | bytes 1540
  129.4 20.9 %all-to-all-start.4 = ((bf16[2,16,5,2048]{3,0,2,1:T(2,128)(2,1)}), bf16[2,16,5,2048]{3,0,2,1:T(2,128)(2,1)}, u32[]{:S(2)}, u32[]{:S(2)}) async-start(bf16[2,16,5,2048]{3,0,2,1:T(2,128)(2,1)} %bitcast.179), calls=%async_computation.4 | async-start | bytes 1310720 | tf_op jit(solution)/shard_map/all_to_all | solution.py:126
Sparse Core Ops, SparseCore 0:
  10.1 78.0 all-gather.1
